TPU v7x, 256 devices: a whole 4x4x8 slice. The times are simulated.
256 devices in a mesh: batch: 4 (over x_hi, core), hidden: 16 (over x_lo, z), width: 4 (over y).
Axes of the slice: x: 4 (x_hi: 2, x_lo: 2; x = x_hi * 2 + x_lo), y: 4, z: 8, core: 2. Of those that a mesh axis runs over, the one named last changes fastest.
Arguments:
- frames: bfloat16 [4, 512, 1280], P('batch', None, 'hidden'), may hold values from -6 to 6
- adapter_weight: bfloat16 [4, 1280, 16384], P(None, 'hidden', 'width'), may hold values from -0.078125 to 0.078125
- text_embed: bfloat16 [512, 16384], P('batch', 'width'), may hold values from -6 to 6
- audio_len: int32 [4], P('batch'), may hold values from 16 to 64, as said below
- text_len: int32 [4], P('batch'), may hold values from 32 to 112, as said below
- norm_gain: bfloat16 [16384], P('width'), may hold values from 0.5 to 1.5
- gate_up: bfloat16 [16384, 2, 26624], P('width', None, ('batch', 'hidden')), may hold values from -0.046875 to 0.046875
- cotangent: bfloat16 [512, 26624], P('width', ('batch', 'hidden')), may hold values from -0.59765625 to 0.59765625
Outputs:
- hidden: bfloat16 [512, 26624], P('width', ('batch', 'hidden'))
- weight_grad: float32 [4, 1280, 16384], P(None, 'hidden', 'width')
Inputs may be any that keep to these rules, and one draw needn't show every extreme that they name: `audio_len`: some sequence holds exactly 16 audio positions and another exactly 64. audio_len + text_len never exceeds 128, and equals it in some sequence.
All inputs are finite; a program needn't handle non-finite values.
Results may differ from a plain program's by a relative error of at most 0.0059.
Values may be sent and summed in bfloat16 or wider, within the bound.
A program may use at most 64 MiB of HBM per device.

v0:
```python
import jax
import jax.numpy as jnp
from jax import lax
from jax.sharding import PartitionSpec as P

D = 16384
norm_eps = 1e-05


def row_lookup(table, row_index):
    slots = jnp.arange(table.shape[0], dtype=jnp.int32)
    return jnp.sum(jnp.where(row_index[:, None] == slots[None, :], table[None, :], 0), axis=1)


def on_device(
    frames, adapter_weight, text_embed, audio_len, text_len, norm_gain, gate_up, cotangent
):
    rows_here, frame_count, feat_here = frames.shape
    seq_len = frame_count // 4
    width_here = adapter_weight.shape[2]
    tok_here = rows_here * seq_len
    stacked = frames.reshape(tok_here, 4 * feat_here)
    kernel = adapter_weight.reshape(4 * feat_here, width_here)
    partial_audio = jnp.dot(stacked, kernel, preferred_element_type=jnp.float32)
    audio_part = lax.psum(partial_audio, "hidden")
    local_index = jnp.arange(tok_here, dtype=jnp.int32)
    row_index = local_index // seq_len
    positions = local_index % seq_len
    audio_count = row_lookup(audio_len, row_index)
    text_count = row_lookup(text_len, row_index)
    is_audio = positions < audio_count
    is_text = jnp.logical_and(jnp.logical_not(is_audio), positions < audio_count + text_count)
    stream = jnp.where(
        is_audio[:, None],
        audio_part,
        jnp.where(is_text[:, None], text_embed.astype(jnp.float32), jnp.zeros_like(audio_part)),
    )
    sum_squares = lax.psum(jnp.sum(stream * stream, axis=1), "width")
    inv_rms = lax.rsqrt(sum_squares / D + norm_eps)
    unit_stream = stream * inv_rms[:, None]
    gain_vals = norm_gain.astype(jnp.float32)
    normed = (unit_stream * gain_vals[None, :]).astype(jnp.bfloat16)
    weights = gate_up.reshape(width_here, -1)
    half_cols = weights.shape[1] // 2
    partial_pair = jnp.dot(
        lax.all_gather(normed, "batch", axis=0, tiled=True),
        weights,
        preferred_element_type=jnp.float32,
    )
    summed = lax.psum_scatter(partial_pair, "width", scatter_dimension=0, tiled=True)
    gate_vals = summed[:, :half_cols]
    up_vals = summed[:, half_cols:]
    sigmoid_gate = jax.nn.sigmoid(gate_vals)
    silu_gate = gate_vals * sigmoid_gate
    hidden = (silu_gate * up_vals).astype(jnp.bfloat16)
    cot_vals = cotangent.astype(jnp.float32)
    silu_slope = sigmoid_gate * (1.0 + gate_vals * (1.0 - sigmoid_gate))
    grad_pair = jnp.concatenate(
        [
            (cot_vals * up_vals * silu_slope).astype(jnp.bfloat16),
            (cot_vals * silu_gate).astype(jnp.bfloat16),
        ],
        axis=1,
    )
    all_pairs = lax.all_gather(grad_pair, "width", axis=0, tiled=True)
    share_rows = tok_here // lax.axis_size("hidden")
    row_block = all_pairs
    normed_grad = lax.psum_scatter(
        lax.dot_general(
            row_block, weights, (((1,), (1,)), ((), ())), preferred_element_type=jnp.float32
        ),
        ("batch", "hidden"),
        scatter_dimension=0,
        tiled=True,
    )
    share_start = lax.axis_index("hidden") * share_rows
    unit_share = lax.dynamic_slice_in_dim(unit_stream, share_start, share_rows, 0)
    inv_share = lax.dynamic_slice_in_dim(inv_rms, share_start, share_rows, 0)
    audio_share = lax.dynamic_slice_in_dim(is_audio, share_start, share_rows, 0)
    scaled_grad = normed_grad * gain_vals[None, :]
    proj_stat = lax.psum(jnp.sum(unit_share * scaled_grad, axis=1), "width") / D
    stream_grad = (scaled_grad - unit_share * proj_stat[:, None]) * inv_share[:, None]
    audio_grad = jnp.where(audio_share[:, None], stream_grad, jnp.zeros_like(stream_grad)).astype(
        jnp.bfloat16
    )
    row_block = stacked
    local_grad = lax.dot_general(
        row_block,
        lax.all_gather(audio_grad, "hidden", axis=0, tiled=True),
        (((0,), (0,)), ((), ())),
        preferred_element_type=jnp.float32,
    )
    weight_grad = lax.psum(local_grad, "batch")
    return (hidden, weight_grad.reshape(4, feat_here, width_here))


def solution(mesh):
    return jax.shard_map(
        on_device,
        mesh=mesh,
        in_specs=(
            P("batch", None, "hidden"),
            P(None, "hidden", "width"),
            P("batch", "width"),
            P("batch"),
            P("batch"),
            P("width"),
            P("width", None, ("batch", "hidden")),
            P("width", ("batch", "hidden")),
        ),
        out_specs=(P("width", ("batch", "hidden")), P(None, "hidden", "width")),
        check_vma=False,
    )
```

profile of v0, /device:TPU:1, one launch (start us, length us, event | category | flops | bytes accessed | tf_op | source)
XLA Modules:
  0.0 757.5 jit_solution(508925325179178368)
XLA Ops:
  7.2 0.0 all-reduce.3.cloned.1.call-start
  7.2 1.2 copy.10
  8.4 0.1 reshape.64
  8.5 0.4 copy-done
  8.9 2.0 fusion.8
  11.0 0.0 all-gather.3.cloned.1.call-start
  11.1 0.6 copy-done.2
  13.0 134.5 %all-reduce.3.cloned.1.call-done = f32[128,4096]{1,0:T(8,128)} async-done(((f32[128,4096]{1,0:T(8,128)}), f32[128,4096]{1,0:T(8,128)}) %all-reduce.3.cloned.1.call-update) | async-done | bytes 2097168 | tf_op jit(solution)/shard_map/psum | solution.py:25
  147.4 2.4 multiply_reduce_fusion
  149.8 8.7 %psum.29 = f32[128]{0:T(128)S(1)} all-reduce(f32[128]{0:T(128)S(1)} %multiply_reduce_fusion), channel_id=1, replica_groups=mesh['batch'=4,'hidden'=16,'width'=4] {'width'}, use_global_device_ids=true, to_apply=%region_2.3 | all-reduce | flops 128 | bytes 1024 | tf_op jit(solution)/shard_map/psum | solution.py:38
  158.5 4.1 multiply_convert_fusion
  162.6 0.0 all-gather.3.cloned.1.call-update
  162.6 0.0 reduce-scatter.3.cloned.1.call-start
  162.7 48.2 %all-gather.3.cloned.1.call-done = bf16[512,4096]{1,0:T(8,128)(2,1)} async-done(((bf16[128,4096]{1,0:T(8,128)(2,1)}), bf16[512,4096]{1,0:T(8,128)(2,1)}) %all-gather.3.cloned.1.call-update) | async-done | bytes 4194320 | tf_op jit(solution)/shard_map/all_gather | solution.py:46
  210.9 9.2 %fusion.9 = f32[512,832]{0,1:T(8,128)} fusion(bf16[512,4096]{1,0:T(8,128)(2,1)} %all-gather.3.cloned.1.call-done, bf16[4096,832]{0,1:T(8,128)(2,1)} %bitcast.19), kind=kOutput, calls=%fused_computation.28 | convolution fusion | flops 3489660928 | bytes 12713984 | tf_op jit(solution)/shard_map/dot_general | solution.py:45
  220.1 0.0 reduce-scatter.5.cloned.1.call-start
  220.1 28.2 %reduce-scatter.3.cloned.1.call-done = f32[128,832]{0,1:T(8,128)} async-done(((f32[512,832]{0,1:T(8,128)}), f32[128,832]{0,1:T(8,128)}) %reduce-scatter.3.cloned.1.call-update) | async-done | bytes 426000 | tf_op jit(solution)/shard_map/reduce_scatter | solution.py:50
  248.3 1.8 fusion.2
  250.1 17.1 %all_gather.10 = bf16[512,832]{0,1:T(8,128)(2,1)S(1)} all-gather(bf16[128,832]{0,1:T(8,128)(2,1)S(1)} %pad_maximum_fusion), channel_id=1, replica_groups=mesh['batch'=4,'hidden'=16,'width'=4] {'width'}, dimensions={0}, use_global_device_ids=true | all-gather | bytes 1064960 | tf_op jit(solution)/shard_map/all_gather | solution.py:65
  267.2 9.7 %fusion.10 = f32[512,4096]{1,0:T(8,128)} fusion(bf16[512,832]{0,1:T(8,128)(2,1)S(1)} %all_gather.10, bf16[4096,832]{0,1:T(8,128)(2,1)} %bitcast.20), kind=kOutput, calls=%fused_computation.29 | convolution fusion | flops 3489660928 | bytes 16056320 | tf_op jit(solution)/shard_map/dot_general | solution.py:69
  276.9 0.0 all-gather.5.cloned.1.call-start
  277.0 0.1 dynamic_slice.9
  277.0 260.5 %reduce-scatter.5.cloned.1.call-done = f32[8,4096]{1,0:T(8,128)} async-done(((f32[512,4096]{1,0:T(8,128)}), f32[8,4096]{1,0:T(8,128)}) %reduce-scatter.5.cloned.1.call-update) | async-done | bytes 131088 | tf_op jit(solution)/shard_map/reduce_scatter | solution.py:68
  537.6 1.1 multiply_reduce_fusion.1
  538.7 0.1 dynamic_slice.11
  538.8 8.8 %psum.30 = f32[8]{0:T(128)S(1)} all-reduce(f32[8]{0:T(128)S(1)} %multiply_reduce_fusion.1), channel_id=1, replica_groups=mesh['batch'=4,'hidden'=16,'width'=4] {'width'}, use_global_device_ids=true, to_apply=%region_6.7 | all-reduce | flops 8 | bytes 64 | tf_op jit(solution)/shard_map/psum | solution.py:81
  547.6 1.7 select_convert_fusion
  549.3 0.0 all-reduce.5.cloned.1.call-start
  549.4 67.9 %all-gather.5.cloned.1.call-done = bf16[128,4096]{1,0:T(8,128)(2,1)} async-done(((bf16[8,4096]{1,0:T(8,128)(2,1)}), bf16[128,4096]{1,0:T(8,128)(2,1)}) %all-gather.5.cloned.1.call-update) | async-done | bytes 1048592 | tf_op jit(solution)/shard_map/all_gather | solution.py:89
  617.3 4.5 fusion.11
  621.8 123.5 %all-reduce.5.cloned.1.call-done = f32[4,80,4096]{2,1,0:T(8,128)} async-done(((f32[4,80,4096]{2,1,0:T(8,128)}), f32[4,80,4096]{2,1,0:T(8,128)}) %all-reduce.5.cloned.1.call-update) | async-done | bytes 5242896 | tf_op jit(solution)/shard_map/psum | solution.py:93
  745.2 5.4 copy.15
  (14 shorter events, 0.1 us)
Async XLA Ops:
  7.2 1.8 copy-start
  7.2 140.3 %all-reduce.3.cloned.1.call-start = ((), (), s32[]{:S(2)}) async-start(), calls=%async_computation.2 | async-start | bytes 4194304 | tf_op jit(solution)/shard_map/psum | solution.py:25
  11.0 0.7 copy-start.2
  11.0 199.9 %all-gather.3.cloned.1.call-start = ((), (), s32[]{:S(2)}) async-start(), calls=%async_computation.3 | async-start | bytes 5242880 | tf_op jit(solution)/shard_map/all_gather | solution.py:46
  162.6 85.7 %reduce-scatter.3.cloned.1.call-start = ((), (), s32[]{:S(2)}) async-start(), calls=%async_computation.4 | async-start | bytes 2129920 | tf_op jit(solution)/shard_map/reduce_scatter | solution.py:50
  210.9 37.4 %copy-start.1 = (bf16[128,416]{0,1:T(8,128)(2,1)S(1)}, bf16[128,416]{0,1:T(8,128)(2,1)}, u32[]{:S(2)}) copy-start(bf16[128,416]{0,1:T(8,128)(2,1)} %param.15) | copy-start | bytes 319492
  220.1 317.5 %reduce-scatter.5.cloned.1.call-start = ((), (), s32[]{:S(2)}) async-start(), calls=%async_computation.5 | async-start | bytes 8519680 | tf_op jit(solution)/shard_map/reduce_scatter | solution.py:68
  276.9 340.4 %all-gather.5.cloned.1.call-start = ((), (), s32[]{:S(2)}) async-start(), calls=%async_computation.6 | async-start | bytes 1114112 | tf_op jit(solution)/shard_map/all_gather | solution.py:89
  549.3 195.9 %all-reduce.5.cloned.1.call-start = ((), (), s32[]{:S(2)}) async-start(), calls=%async_computation.7 | async-start | bytes 10485760 | tf_op jit(solution)/shard_map/psum | solution.py:93
Sparse Core Ops, SparseCore 0:
  11.2 136.1 all-reduce.2
  162.8 48.0 all-gather.2
  220.2 28.0 reduce-scatter.2
  277.0 260.5 reduce-scatter.4
  549.4 67.7 all-gather.4
  621.9 123.2 all-reduce.4
where the time goes:
time: 758 us
  waiting for transfers between devices  663 us (87%)
  blocking collectives  34.6 us (5%)
  matrix products  25.3 us (3%)
  between operations  15.5 us (2%)
  other arithmetic  11.1 us (1%)
  local copies, waits for them, and re-layouts  7.94 us (1%)
    reduce_scatter x1, waiting for transfers between devices, on_device(): lax.psum_scatter(lax.dot_general(row_block, weights, (((1,), (1,)), ((),...  261 us
    psum x1, waiting for transfers between devices, on_device(): audio_part = lax.psum(partial_audio, 'hidden')  134 us
    psum x1, waiting for transfers between devices, on_device(): weight_grad = lax.psum(local_grad, 'batch')  123 us
    all_gather x1, waiting for transfers between devices, on_device(): lax.all_gather(audio_grad, 'hidden', axis=0, tiled=True)  67.9 us
    all_gather x1, waiting for transfers between devices, on_device(): lax.all_gather(normed, 'batch', axis=0, tiled=True)  48.2 us
    reduce_scatter x1, waiting for transfers between devices, on_device(): lax.psum_scatter(partial_pair, 'width', scatter_dimension=0, tiled=True)  28.2 us
    all_gather x1, blocking collectives, on_device(): all_pairs = lax.all_gather(grad_pair, 'width', axis=0, tiled=True)  17.1 us
  transfers between devices with their start and end apart: 6, of which 6 were waited for; matrix products, arithmetic and copies ran while one was open for 0% of the time, Pallas kernels for 0%

commit v1 on v0

--- a/solution.py
+++ b/solution.py
@@ -90,7 +90,8 @@
         (((0,), (0,)), ((), ())),
         preferred_element_type=jnp.float32,
     )
-    weight_grad = lax.psum(local_grad, "batch")
+    shards = lax.all_gather(local_grad, "batch", axis=0, tiled=False)
+    weight_grad = shards.sum(axis=0)
     return (hidden, weight_grad.reshape(4, feat_here, width_here))
 
 

time: 758 us -> 786 us (1.037)
  waiting for transfers between devices: 663 us -> 686 us
  other arithmetic: 11.1 us -> 21.5 us
    all_gather x0 -> x1, waiting for transfers between devices: none -> 147 us  [on_device(): shards = lax.all_gather(local_grad, 'batch', axis=0, tiled=False)]
    psum x1 -> x0, waiting for transfers between devices: 123 us -> none  [on_device(): weight_grad = lax.psum(local_grad, 'batch')]
    reduce_sum x0 -> x1, other arithmetic: none -> 10.8 us  [on_device(): weight_grad = shards.sum(axis=0)]
where the time goes in v1:
time: 786 us; the launch traced here: 785 us
  waiting for transfers between devices  686 us (87%)
  blocking collectives  35 us (4%)
  matrix products  25.4 us (3%)
  other arithmetic  21.5 us (3%)
  between operations  15.5 us (2%)
    reduce_scatter x1, waiting for transfers between devices, on_device(): lax.psum_scatter(lax.dot_general(row_block, weights, (((1,), (1,)), ((),...  260 us
    all_gather x1, waiting for transfers between devices, on_device(): shards = lax.all_gather(local_grad, 'batch', axis=0, tiled=False)  147 us
    psum x1, waiting for transfers between devices, on_device(): audio_part = lax.psum(partial_audio, 'hidden')  135 us
    all_gather x1, waiting for transfers between devices, on_device(): lax.all_gather(audio_grad, 'hidden', axis=0, tiled=True)  67.6 us
    all_gather x1, waiting for transfers between devices, on_device(): lax.all_gather(normed, 'batch', axis=0, tiled=True)  48 us
    reduce_scatter x1, waiting for transfers between devices, on_device(): lax.psum_scatter(partial_pair, 'width', scatter_dimension=0, tiled=True)  28.2 us
    all_gather x1, blocking collectives, on_device(): all_pairs = lax.all_gather(grad_pair, 'width', axis=0, tiled=True)  17 us
  transfers between devices with their start and end apart: 6, of which 6 were waited for; matrix products, arithmetic and copies ran while one was open for 0% of the time, Pallas kernels for 0%

profile of v1, /device:TPU:1, one launch (start us, length us, event | category | flops | bytes accessed | tf_op | source)
XLA Modules:
  0.0 785.4 jit_solution(14353860121901255536)
XLA Ops:
  7.2 0.0 all-reduce.2.cloned.1.call-start
  7.2 1.2 copy.10
  8.4 0.1 reshape.64
  8.5 0.4 copy-done
  9.0 2.0 fusion.8
  11.0 0.0 all-gather.5.cloned.1.call-start
  12.4 135.1 %all-reduce.2.cloned.1.call-done = f32[128,4096]{1,0:T(8,128)} async-done(((f32[128,4096]{1,0:T(8,128)}), f32[128,4096]{1,0:T(8,128)}) %all-reduce.2.cloned.1.call-update) | async-done | bytes 2097168 | tf_op jit(solution)/shard_map/psum | solution.py:25
  147.5 2.5 multiply_reduce_fusion
  150.0 8.9 %psum.22 = f32[128]{0:T(128)S(1)} all-reduce(f32[128]{0:T(128)S(1)} %multiply_reduce_fusion), channel_id=1, replica_groups=mesh['batch'=4,'hidden'=16,'width'=4] {'width'}, use_global_device_ids=true, to_apply=%region_2.3 | all-reduce | flops 128 | bytes 1024 | tf_op jit(solution)/shard_map/psum | solution.py:38
  158.8 3.5 multiply_convert_fusion
  162.3 0.0 all-gather.5.cloned.1.call-update
  162.4 0.0 reduce-scatter.3.cloned.1.call-start
  162.4 48.0 %all-gather.5.cloned.1.call-done = bf16[512,4096]{1,0:T(8,128)(2,1)} async-done(((bf16[128,4096]{1,0:T(8,128)(2,1)}), bf16[512,4096]{1,0:T(8,128)(2,1)}) %all-gather.5.cloned.1.call-update) | async-done | bytes 4194320 | tf_op jit(solution)/shard_map/all_gather | solution.py:46
  210.4 9.2 %fusion.9 = f32[512,832]{0,1:T(8,128)} fusion(bf16[512,4096]{1,0:T(8,128)(2,1)} %all-gather.5.cloned.1.call-done, bf16[4096,832]{0,1:T(8,128)(2,1)} %bitcast.20), kind=kOutput, calls=%fused_computation.29 | convolution fusion | flops 3489660928 | bytes 12713984 | tf_op jit(solution)/shard_map/dot_general | solution.py:45
  219.6 0.0 reduce-scatter.3.cloned.1.call-update
  219.6 0.0 reduce-scatter.5.cloned.1.call-start
  219.7 28.2 %reduce-scatter.3.cloned.1.call-done = f32[128,832]{0,1:T(8,128)} async-done(((f32[512,832]{0,1:T(8,128)}), f32[128,832]{0,1:T(8,128)}) %reduce-scatter.3.cloned.1.call-update) | async-done | bytes 426000 | tf_op jit(solution)/shard_map/reduce_scatter | solution.py:50
  247.8 1.8 fusion.2
  249.7 17.0 %all_gather.16 = bf16[512,832]{0,1:T(8,128)(2,1)S(1)} all-gather(bf16[128,832]{0,1:T(8,128)(2,1)S(1)} %pad_maximum_fusion), channel_id=1, replica_groups=mesh['batch'=4,'hidden'=16,'width'=4] {'width'}, dimensions={0}, use_global_device_ids=true | all-gather | bytes 1064960 | tf_op jit(solution)/shard_map/all_gather | solution.py:65
  266.7 9.7 %fusion.10 = f32[512,4096]{1,0:T(8,128)} fusion(bf16[512,832]{0,1:T(8,128)(2,1)S(1)} %all_gather.16, bf16[4096,832]{0,1:T(8,128)(2,1)} %bitcast.21), kind=kOutput, calls=%fused_computation.30 | convolution fusion | flops 3489660928 | bytes 16056320 | tf_op jit(solution)/shard_map/dot_general | solution.py:69
  276.4 0.0 all-gather.7.cloned.1.call-start
  276.5 0.1 dynamic_slice.9
  276.6 260.5 %reduce-scatter.5.cloned.1.call-done = f32[8,4096]{1,0:T(8,128)} async-done(((f32[512,4096]{1,0:T(8,128)}), f32[8,4096]{1,0:T(8,128)}) %reduce-scatter.5.cloned.1.call-update) | async-done | bytes 131088 | tf_op jit(solution)/shard_map/reduce_scatter | solution.py:68
  537.0 1.1 multiply_reduce_fusion.1
  538.1 0.1 dynamic_slice.11
  538.2 9.1 %psum.23 = f32[8]{0:T(128)S(1)} all-reduce(f32[8]{0:T(128)S(1)} %multiply_reduce_fusion.1), channel_id=1, replica_groups=mesh['batch'=4,'hidden'=16,'width'=4] {'width'}, use_global_device_ids=true, to_apply=%region_6.7 | all-reduce | flops 8 | bytes 64 | tf_op jit(solution)/shard_map/psum | solution.py:81
  547.3 1.7 select_convert_fusion
  549.0 0.0 all-gather.9.cloned.1.call-start
  549.0 67.6 %all-gather.7.cloned.1.call-done = bf16[128,4096]{1,0:T(8,128)(2,1)} async-done(((bf16[8,4096]{1,0:T(8,128)(2,1)}), bf16[128,4096]{1,0:T(8,128)(2,1)}) %all-gather.7.cloned.1.call-update) | async-done | bytes 1048592 | tf_op jit(solution)/shard_map/all_gather | solution.py:89
  616.6 4.5 convolution_bitcast_fusion
  621.1 146.6 %all-gather.9.cloned.1.call-done = f32[1280,4096]{1,0:T(8,128)} async-done(((f32[320,4096]{1,0:T(8,128)}), f32[1280,4096]{1,0:T(8,128)}) %all-gather.9.cloned.1.call-update) | async-done | bytes 20971536 | tf_op jit(solution)/shard_map/all_gather | solution.py:93
  767.7 10.8 %reduce_sum.29 = f32[320,4096]{1,0:T(8,128)} reduce(f32[4,320,4096]{2,1,0:T(8,128)} %bitcast.19, f32[]{:T(128)} %constant.56.clone.1), dimensions={0}, to_apply=%region_7.8 | reduce | flops 3932160 | bytes 26214404 | tf_op jit(solution)/shard_map/reduce_sum | solution.py:94
  (18 shorter events, 0.1 us)
Async XLA Ops:
  7.2 1.8 copy-start
  7.2 140.3 %all-reduce.2.cloned.1.call-start = ((), (), s32[]{:S(2)}) async-start(), calls=%async_computation.2 | async-start | bytes 4194304 | tf_op jit(solution)/shard_map/psum | solution.py:25
  11.0 1.4 copy-start.4
  11.0 199.4 %all-gather.5.cloned.1.call-start = ((), (), s32[]{:S(2)}) async-start(), calls=%async_computation.3 | async-start | bytes 5242880 | tf_op jit(solution)/shard_map/all_gather | solution.py:46
  147.4 11.4 %copy-start.2 = (f32[128,4096]{1,0:T(8,128)S(1)}, f32[128,4096]{1,0:T(8,128)}, u32[]{:S(2)}) copy-start(f32[128,4096]{1,0:T(8,128)} %all-reduce.2.cloned.1.call-done) | copy-start | bytes 6291460
  162.4 85.5 %reduce-scatter.3.cloned.1.call-start = ((), (), s32[]{:S(2)}) async-start(), calls=%async_computation.4 | async-start | bytes 2129920 | tf_op jit(solution)/shard_map/reduce_scatter | solution.py:50
  210.4 37.4 %copy-start.3 = (bf16[128,416]{0,1:T(8,128)(2,1)S(1)}, bf16[128,416]{0,1:T(8,128)(2,1)}, u32[]{:S(2)}) copy-start(bf16[128,416]{0,1:T(8,128)(2,1)} %param.15) | copy-start | bytes 319492
  219.6 317.4 %reduce-scatter.5.cloned.1.call-start = ((), (), s32[]{:S(2)}) async-start(), calls=%async_computation.5 | async-start | bytes 8519680 | tf_op jit(solution)/shard_map/reduce_scatter | solution.py:68
  276.4 340.2 %all-gather.7.cloned.1.call-start = ((), (), s32[]{:S(2)}) async-start(), calls=%async_computation.6 | async-start | bytes 1114112 | tf_op jit(solution)/shard_map/all_gather | solution.py:89
  549.0 218.7 %all-gather.9.cloned.1.call-start = ((), (), s32[]{:S(2)}) async-start(), calls=%async_computation.7 | async-start | bytes 26214400 | tf_op jit(solution)/shard_map/all_gather | solution.py:93
  767.7 10.8 %copy-start.1 = (bf16[4,80,4096]{2,1,0:T(8,128)(2,1)S(1)}, bf16[4,80,4096]{2,1,0:T(8,128)(2,1)}, u32[]{:S(2)}) copy-start(bf16[4,80,4096]{2,1,0:T(8,128)(2,1)} %param.9) | copy-start | bytes 7864324
Sparse Core Ops, SparseCore 0:
  11.2 136.1 all-reduce.1
  162.5 47.8 all-gather.4
  219.7 28.0 reduce-scatter.2
  276.5 260.4 reduce-scatter.4
  549.1 67.4 all-gather.6
  621.2 146.4 all-gather.8
